TPU v7x, 256 devices: a whole 4x4x8 slice. The times are simulated.
256 devices in a mesh: sec: 2 (over y_lo), grp: 16 (over z, y_hi), tp: 8 (over x, core).
Axes of the slice: x: 4, y: 4 (y_hi: 2, y_lo: 2; y = y_hi * 2 + y_lo), z: 8, core: 2. Of those that a mesh axis runs over, the one named last changes fastest.
Arguments:
- hidden_in: bfloat16 [1024, 7168], P(('sec', 'grp', 'tp')), may hold values from -6 to 6
- queries: bfloat16 [1024, 16, 8, 576], P(('sec', 'grp'), None, 'tp'), may hold values from -61 to 61
- latent_cache: bfloat16 [1024, 64, 576], P(('sec', 'grp')), may hold values from -6 to 6
- lengths: int32 [1024], P(('sec', 'grp')), may hold values from 2 to 64, as said below
- w_uv: bfloat16 [16, 8, 512, 128], P(None, 'tp'), may hold values from -0.75 to 0.75
- attn_weight: bfloat16 [16, 8, 128, 7168], P(None, 'tp', None, 'grp'), may hold values from -0.125 to 0.125
- norm_gain: float32 [7168], replicated, may hold values from 0.1 to 1.9
- router: bfloat16 [7168, 32], replicated, may hold values from -0.0625 to 0.0625
- routes: int32 [1024, 8], P(('sec', 'grp', 'tp')), may hold values from 0 to 31, all different within a row; in each aligned block of 4 rows (0 to 3, 4 to 7, ...) at most 2 rows name the same one
- live_counts: int32 [256], P(('sec', 'grp', 'tp')), may hold values from 3 to 4, as said below
- expert_in: bfloat16 [32, 7168, 2, 1024], P(('sec', 'grp'), None, None, 'tp'), may hold values from -0.0625 to 0.0625
- expert_out: bfloat16 [32, 1024, 7168], P(('sec', 'grp'), 'tp'), may hold values from -0.5 to 0.5
Outputs:
- layer_out: bfloat16 [1024, 7168], P(('sec', 'grp', 'tp'))
Inputs may be any that keep to these rules, and one draw needn't show every extreme that they name: `lengths`: some request has exactly 64 cached positions and some has 2. `live_counts`: some device has all 4 slots live and some has exactly 3. `routes`: the 8 experts of a token differ. Within the rows of one device (aligned blocks of 4 rows) no expert is named by more than 2 rows, a bound that some block reaches.
All inputs are finite; a program needn't handle non-finite values.
Results may differ from a plain program's by a relative error of at most 0.018.
Values may be sent and summed in bfloat16 or wider, within the bound.
No kernel may reach another device: no remote copies, remote signals or barrier semaphores. Data moves between devices by JAX's collectives and lax.ppermute only.
A program may use at most 64 MiB of HBM per device.

v0:
```python
import jax
import jax.numpy as jnp
from jax import lax
from jax.sharding import Mesh
from jax.sharding import PartitionSpec as P

GRP = ("grp_0", "grp_1")
SEC_GRP = ("sec", "grp_0", "grp_1")
GRP_SEC = ("grp_0", "grp_1", "sec")
SEC_GRP_TP = ("sec", "grp_0", "grp_1", "tp")
score_scale = 192.0 ** (-0.5)
route_scale = 2.5


def gathered_by_axis(x, axes, dim):
    out = x
    for number in range(len(axes) - 1, -1, -1):
        out = lax.all_gather(out, axes[number], axis=dim, tiled=True)
    return out


def in_blocks(x, dim, peers):
    lengths = x.shape
    tiles = x.reshape(*lengths[:dim], peers, lengths[dim] // peers, *lengths[dim + 1 :])
    return jnp.moveaxis(tiles, dim, 0)


def sent_and_summed(x, axis, dim):
    tiles = in_blocks(x, dim, lax.axis_size(axis))
    arrived = lax.all_to_all(tiles, axis, split_axis=0, concat_axis=0, tiled=True)
    return arrived.astype(jnp.float32).sum(axis=0)


def in_order(tiles, dim):
    tiles = jnp.moveaxis(tiles, 0, dim)
    lengths = tiles.shape
    return tiles.reshape(*lengths[:dim], lengths[dim] * lengths[dim + 1], *lengths[dim + 2 :])


def exchange_both(x, axis, axes, splits, concats):
    sizes = [lax.axis_size(a) for a in axes]
    tiles = in_blocks(x, splits[0], sizes[0])
    tiles = jnp.moveaxis(in_blocks(tiles, splits[1] + 1, sizes[1]), 0, 1)
    inside = tiles.shape[2:]
    tiles = tiles.reshape(-1, *inside)
    tiles = lax.all_to_all(tiles, axis, split_axis=0, concat_axis=0, tiled=True)
    tiles = in_order(tiles.reshape(*sizes, *inside), concats[0] + 1)
    return in_order(tiles, concats[1])


def expert_slice(rows_in, expert_in, expert_out):
    width = rows_in.shape[1]
    slice_width = expert_in.shape[3]
    gate_up = jnp.dot(
        rows_in, expert_in[0].reshape(width, 2 * slice_width), preferred_element_type=jnp.float32
    )
    activated = (jax.nn.silu(gate_up[:, :slice_width]) * gate_up[:, slice_width:]).astype(
        jnp.bfloat16
    )
    return jnp.dot(activated, expert_out[0], preferred_element_type=jnp.float32).astype(
        jnp.bfloat16
    )


def shards(
    hidden_in,
    queries,
    latent_cache,
    lengths,
    w_uv,
    attn_weight,
    norm_gain,
    router,
    routes,
    live_counts,
    expert_in,
    expert_out,
):
    count_of_tokens, width = hidden_in.shape
    sections = lax.axis_size("sec")
    expert_groups = lax.axis_size(GRP)
    slices = lax.axis_size("tp")
    latent_width = w_uv.shape[2]
    query_block = queries[:, :, 0, :]
    scores = (
        jnp.einsum("bhr,bpr->bhp", query_block, latent_cache, preferred_element_type=jnp.float32)
        * score_scale
    )
    positions = jnp.arange(latent_cache.shape[1])
    visible = positions[None, None, :] < lengths[:, None, None]
    scores = jnp.where(visible, scores, -1e30)
    highest = jnp.max(scores, axis=2, keepdims=True)
    raised = jnp.exp(scores - highest)
    softmax_weights = (raised / jnp.sum(raised, axis=2, keepdims=True)).astype(jnp.bfloat16)
    latent_out = jnp.einsum(
        "bhp,bpc->bhc",
        softmax_weights,
        latent_cache[:, :, :latent_width],
        preferred_element_type=jnp.float32,
    ).astype(jnp.bfloat16)
    head_out = jnp.einsum(
        "bhc,hcv->bhv", latent_out, w_uv[:, 0], preferred_element_type=jnp.float32
    ).astype(jnp.bfloat16)
    head_rows = head_out.reshape(head_out.shape[0], -1)
    out_block = attn_weight[:, 0].reshape(-1, attn_weight.shape[3])
    partial_value = jnp.dot(
        gathered_by_axis(head_rows, GRP, 0), out_block, preferred_element_type=jnp.float32
    )
    partial_value = partial_value.reshape(
        expert_groups, slices, count_of_tokens, partial_value.shape[1]
    )
    summed = sent_and_summed(partial_value.astype(jnp.bfloat16), "tp", 1)
    column_part = summed[:, 0].astype(jnp.bfloat16)
    attention = lax.all_to_all(column_part, GRP, split_axis=0, concat_axis=2, tiled=True)[0]
    residual = hidden_in.astype(jnp.float32) + attention.astype(jnp.float32)
    normalized_input = (
        residual
        * lax.rsqrt(jnp.mean(residual * residual, axis=1, keepdims=True) + 1e-06)
        * norm_gain
    ).astype(jnp.bfloat16)
    experts = router.shape[1]
    per_token = routes.shape[1]
    capacity = max(2, 2 * count_of_tokens * per_token // experts)
    affinity = jax.nn.sigmoid(jnp.dot(normalized_input, router, preferred_element_type=jnp.float32))
    picked = routes[:, :, None] == jnp.arange(experts)[None, None, :]
    chosen = jnp.sum(jnp.where(picked, affinity[:, None, :], 0.0), axis=2)
    living = jnp.arange(count_of_tokens) < live_counts[0]
    gate_weights = (
        route_scale
        * chosen
        / jnp.sum(chosen, axis=1, keepdims=True)
        * living[:, None].astype(jnp.float32)
    )
    routed = jnp.any(picked, axis=1) & living[:, None]
    routed_count = routed.astype(jnp.int32)
    slot_index = jnp.cumsum(routed_count, axis=0) - routed_count
    placed_tokens = routed[:, :, None] & (
        slot_index[:, :, None] == jnp.arange(capacity)[None, None, :]
    )
    expert_gate = jnp.sum(jnp.where(picked, gate_weights[:, :, None], 0.0), axis=1)
    outgoing = jnp.einsum(
        "poy,pj->oyj",
        placed_tokens.astype(jnp.bfloat16),
        normalized_input,
        preferred_element_type=jnp.float32,
    ).astype(jnp.bfloat16)
    combine_rows = (placed_tokens.astype(jnp.float32) * expert_gate[:, :, None]).reshape(
        count_of_tokens, experts * capacity
    )
    once_rows = outgoing.reshape(sections, expert_groups, capacity, width)
    arrived = exchange_both(once_rows, SEC_GRP, ("sec", GRP), (0, 1), (0, 1))
    local_rows = arrived.reshape(-1, width)
    every_out = expert_slice(
        lax.all_gather(local_rows, "tp", axis=0, tiled=True), expert_in, expert_out
    )
    own_sums = lax.psum_scatter(
        every_out.astype(jnp.float32).astype(jnp.bfloat16), "tp", scatter_dimension=0, tiled=True
    ).astype(jnp.float32)
    own_sums = own_sums.reshape(sections, expert_groups, capacity, width)
    back_rows = exchange_both(
        own_sums.astype(jnp.bfloat16), GRP_SEC, (GRP, "sec"), (1, 0), (1, 0)
    ).astype(own_sums.dtype)
    expert_sums = back_rows.reshape(experts * capacity, width)
    expert_mix = jnp.dot(combine_rows, expert_sums, precision=lax.Precision.HIGHEST)
    return (residual + expert_mix).astype(jnp.bfloat16)


def solution(mesh):
    torus = Mesh(
        mesh.devices.reshape(mesh.shape["sec"], 8, 2, mesh.shape["tp"]),
        ("sec", "grp_0", "grp_1", "tp"),
    )
    in_specs = (
        P(SEC_GRP_TP, None),
        P(SEC_GRP, None, "tp", None),
        P(SEC_GRP, None, None),
        P(SEC_GRP),
        P(None, "tp", None, None),
        P(None, "tp", None, GRP),
        P(),
        P(),
        P(SEC_GRP_TP, None),
        P(SEC_GRP_TP),
        P(SEC_GRP, None, None, "tp"),
        P(SEC_GRP, "tp", None),
    )
    out_specs = P(SEC_GRP_TP, None)
    return jax.shard_map(
        shards, mesh=torus, in_specs=in_specs, out_specs=out_specs, check_vma=False
    )
```

profile of v0, /device:TPU:8, one launch (start us, length us, event | category | flops | bytes accessed | tf_op | source)
XLA Modules:
  0.0 292.9 jit_solution(1517495895846176154)
XLA Ops:
  6.5 0.0 copy-start
  6.5 0.0 all-gather.3.cloned.1.call-start
  6.5 0.9 iota_compare_fusion.1
  7.4 2.9 fusion.29
  10.3 0.2 fusion.52
  10.5 2.5 fusion.19
  13.1 0.0 copy-done
  13.1 0.6 fusion.33
  13.7 7.5 %all_gather.9 = bf16[64,2048]{1,0:T(8,128)(2,1)} all-gather(bf16[32,2048]{1,0:T(8,128)(2,1)S(1)} %bitcast.86), channel_id=1, replica_groups=mesh['sec'=2,'grp_0'=8,'grp_1'=2,'tp'=8] {'grp_1'}, dimensions={0}, use_global_device_ids=true | all-gather | bytes 393216 | tf_op jit(solution)/shard_map/all_gather | solution.py:18
  21.3 0.0 all-gather.3.cloned.1.call-update
  21.9 3.9 %copy.34 = bf16[16,1,128,448]{2,0,3,1:T(8,128)(2,1)} copy(bf16[16,1,128,448]{2,3,1,0:T(8,128)(2,1)} %param.17) | data formatting | bytes 3670016 | tf_op args[5]
  25.9 3.9 %reshape.224 = bf16[2048,448,1,1]{0,1,2,3:T(8,128)(2,1)} reshape(bf16[16,1,128,448]{2,0,3,1:T(8,128)(2,1)} %copy.34) | data formatting | bytes 3670016 | tf_op jit(solution)/shard_map/reshape;squeeze | solution.py:105
  29.7 35.4 %all-gather.3.cloned.1.call-done = bf16[512,2048]{1,0:T(8,128)(2,1)} async-done(((bf16[64,2048]{1,0:T(8,128)(2,1)}), bf16[512,2048]{1,0:T(8,128)(2,1)}) %all-gather.3.cloned.1.call-update) | async-done | bytes 2097168 | tf_op jit(solution)/shard_map/all_gather | solution.py:18
  65.2 4.1 %dot_general.32 = bf16[16,8,4,2048]{3,2,1,0:T(4,128)(2,1)} reshape(bf16[512,2048]{1,0:T(8,128)(2,1)} %all-gather.3.cloned.1.call-done) | data formatting | bytes 4194304 | tf_op jit(solution)/shard_map/dot_general | solution.py:106
  69.3 3.6 %fusion.22 = bf16[8,16,1,4,448]{4,0,3,1,2:T(8,128)(2,1)S(1)} fusion(bf16[2048,448,1,1]{0,1,2,3:T(8,128)(2,1)} %reshape.224, bf16[16,8,4,2048]{3,2,1,0:T(4,128)(2,1)} %dot_general.32), kind=kOutput, calls=%fused_computation.19 | convolution fusion | flops 939753472 | bytes 4390912 | tf_op jit(solution)/shard_map/dot_general | solution.py:106
  72.9 0.0 copy-start.4
  72.9 0.0 copy-start.2
  72.9 0.0 copy-start.3
  72.9 1.1 copy.36
  74.0 4.3 %all-to-all-start = ((bf16[8,16,1,4,448]{4,3,1,2,0:T(4,128)(2,1)}), bf16[8,16,1,4,448]{4,3,1,2,0:T(4,128)(2,1)S(1)}, u32[]{:S(2)}, u32[]{:S(2)}) async-start(bf16[8,16,1,4,448]{4,3,1,2,0:T(4,128)(2,1)} %copy.36), calls=%async_computation | async-start | bytes 1048576 | tf_op jit(solution)/shard_map/all_to_all | solution.py:30
  78.2 0.0 copy-done.4
  78.2 0.1 fusion.47
  78.3 0.1 fusion.51
  78.5 10.1 %all-to-all-done = bf16[8,16,1,4,448]{4,3,1,2,0:T(4,128)(2,1)S(1)} async-done(((bf16[8,16,1,4,448]{4,3,1,2,0:T(4,128)(2,1)}), bf16[8,16,1,4,448]{4,3,1,2,0:T(4,128)(2,1)S(1)}, u32[]{:S(2)}, u32[]{:S(2)}) %all-to-all-start) | async-done | bytes 458784 | tf_op jit(solution)/shard_map/all_to_all | solution.py:30
  88.5 0.9 reduce_sum.58
  89.4 5.9 %all-to-all-start.1 = ((bf16[16,4,448]{2,1,0:T(4,128)(2,1)}), bf16[16,4,448]{2,1,0:T(4,128)(2,1)S(1)}, u32[]{:S(2)}, u32[]{:S(2)}) async-start(bf16[16,4,448]{2,1,0:T(4,128)(2,1)} %reduce_sum.58), calls=%async_computation.1 | async-start | bytes 131072 | tf_op jit(solution)/shard_map/all_to_all | solution.py:114
  95.4 0.0 all-gather.5.cloned.1.call-start
  95.4 0.1 copy.39
  95.5 0.1 copy.40
  95.6 10.3 %all-to-all-done.1 = bf16[16,4,448]{2,1,0:T(4,128)(2,1)S(1)} async-done(((bf16[16,4,448]{2,1,0:T(4,128)(2,1)}), bf16[16,4,448]{2,1,0:T(4,128)(2,1)S(1)}, u32[]{:S(2)}, u32[]{:S(2)}) %all-to-all-start.1) | async-done | bytes 57376 | tf_op jit(solution)/shard_map/all_to_all | solution.py:114
  106.0 0.1 reshape.222
  106.1 0.0 copy-done.2
  106.1 0.2 multiply_reduce_fusion
  106.3 0.0 copy-done.3
  106.3 0.1 multiply_convert_fusion
  106.4 1.2 fusion.38
  107.7 0.2 select_reduce_fusion
  107.9 0.1 divide_multiply_fusion
  107.9 0.1 select_reduce_fusion.2
  108.0 0.1 copy.41
  108.2 0.4 fusion.1
  108.6 0.9 copy.43
  109.5 27.3 %all_to_all.24 = bf16[32,1,1,2,7168]{4,3,2,1,0:T(2,128)(2,1)S(1)} all-to-all(bf16[32,1,1,2,7168]{4,3,2,1,0:T(2,128)(2,1)S(1)} %copy.43), channel_id=1, replica_groups=mesh['sec'=2,'grp_0'=8,'grp_1'=2,'tp'=8] {'sec','grp_0','grp_1'}, dimensions={0} | all-to-all | bytes 1835008 | tf_op jit(solution)/shard_map/all_to_all | solution.py:46
  136.9 1.3 reshape_reshape.7
  138.1 0.0 all-gather.5.cloned.1.call-update
  138.1 0.2 reduce-scatter.2.cloned.1.call-start
  138.4 43.3 %all-gather.5.cloned.1.call-done = bf16[512,7168]{1,0:T(8,128)(2,1)} async-done(((bf16[64,7168]{1,0:T(8,128)(2,1)}), bf16[512,7168]{1,0:T(8,128)(2,1)}) %all-gather.5.cloned.1.call-update) | async-done | bytes 7340048 | tf_op jit(solution)/shard_map/all_gather | solution.py:154
  181.7 0.0 copy-start.1
  181.7 6.3 %fusion.3 = f32[512,256]{1,0:T(8,128)S(1)} fusion(bf16[512,7168]{1,0:T(8,128)(2,1)} %all-gather.5.cloned.1.call-done, bf16[896,8,2,128]{3,2,1,0:T(2,128)(2,1)} %bitcast.88), kind=kOutput, calls=%fused_computation.6 | convolution fusion | flops 1879048192 | bytes 11534336 | tf_op jit(solution)/shard_map/dot_general | solution.py:54
  188.0 0.0 copy-done.1
  188.0 5.1 %convolution_convert_fusion = bf16[512,7168]{1,0:T(8,128)(2,1)} fusion(bf16[1,128,7168]{2,1,0:T(8,128)(2,1)S(1)} %copy-done.1, f32[512,256]{1,0:T(8,128)S(1)} %fusion.3), kind=kOutput, calls=%fused_computation.1 | convolution fusion | flops 943587328 | bytes 9699328 | tf_op jit(solution)/shard_map/dot_general | solution.py:60
  193.1 0.0 reduce-scatter.2.cloned.1.call-update
  193.1 50.3 %reduce-scatter.2.cloned.1.call-done = bf16[64,7168]{1,0:T(8,128)(2,1)} async-done(((bf16[512,7168]{1,0:T(8,128)(2,1)}), bf16[64,7168]{1,0:T(8,128)(2,1)}) %reduce-scatter.2.cloned.1.call-update) | async-done | bytes 917520 | tf_op jit(solution)/shard_map/reduce_scatter | solution.py:156
  243.5 2.3 convert_element_type.99
  245.8 0.6 copy.44
  246.4 34.7 %all_to_all.25 = bf16[32,1,1,2,7168]{4,3,2,1,0:T(2,128)(2,1)S(1)} all-to-all(bf16[32,1,1,2,7168]{4,3,2,1,0:T(2,128)(2,1)S(1)} %bitcast.83), channel_id=1, replica_groups=mesh['sec'=2,'grp_0'=8,'grp_1'=2,'tp'=8] {'grp_0','grp_1','sec'}, dimensions={0} | all-to-all | bytes 1835008 | tf_op jit(solution)/shard_map/all_to_all | solution.py:46
  281.1 1.6 copy.67
  282.7 2.5 reshape.221
  285.2 1.2 fusion.2
  (8 shorter events, 0.2 us)
Async XLA Ops:
  6.5 6.6 %copy-start = (bf16[16,1,512,128]{3,2,1,0:T(8,128)(2,1)S(1)}, bf16[16,1,512,128]{3,2,1,0:T(8,128)(2,1)}, u32[]{:S(2)}) copy-start(bf16[16,1,512,128]{3,2,1,0:T(8,128)(2,1)} %param.16) | copy-start | bytes 6291460
  6.5 58.6 %all-gather.3.cloned.1.call-start = ((), (), s32[]{:S(2)}) async-start(), calls=%async_computation.5 | async-start | bytes 2359296 | tf_op jit(solution)/shard_map/all_gather | solution.py:18
  72.9 5.4 %copy-start.4 = (s32[4,8]{1,0:T(4,128)S(1)}, s32[4,8]{1,0:T(4,128)}, u32[]{:S(2)}) copy-start(s32[4,8]{1,0:T(4,128)} %param.20) | copy-start | bytes 388
  72.9 33.2 %copy-start.2 = (bf16[4,7168]{1,0:T(4,128)(2,1)S(1)}, bf16[4,7168]{1,0:T(4,128)(2,1)}, u32[]{:S(2)}) copy-start(bf16[4,7168]{1,0:T(4,128)(2,1)} %param.12) | copy-start | bytes 172036
  72.9 33.4 %copy-start.3 = (f32[7168]{0:T(1024)S(1)}, f32[7168]{0:T(1024)}, u32[]{:S(2)}) copy-start(f32[7168]{0:T(1024)} %param.18) | copy-start | bytes 86020
  74.0 14.6 %all-to-all-start = ((bf16[8,16,1,4,448]{4,3,1,2,0:T(4,128)(2,1)}), bf16[8,16,1,4,448]{4,3,1,2,0:T(4,128)(2,1)S(1)}, u32[]{:S(2)}, u32[]{:S(2)}) async-start(bf16[8,16,1,4,448]{4,3,1,2,0:T(4,128)(2,1)} %copy.36), calls=%async_computation | async-start | bytes 1048576 | tf_op jit(solution)/shard_map/all_to_all | solution.py:30
  89.4 16.5 %all-to-all-start.1 = ((bf16[16,4,448]{2,1,0:T(4,128)(2,1)}), bf16[16,4,448]{2,1,0:T(4,128)(2,1)S(1)}, u32[]{:S(2)}, u32[]{:S(2)}) async-start(bf16[16,4,448]{2,1,0:T(4,128)(2,1)} %reduce_sum.58), calls=%async_computation.1 | async-start | bytes 131072 | tf_op jit(solution)/shard_map/all_to_all | solution.py:114
  95.4 86.3 %all-gather.5.cloned.1.call-start = ((), (), s32[]{:S(2)}) async-start(), calls=%async_computation.6 | async-start | bytes 8257536 | tf_op jit(solution)/shard_map/all_gather | solution.py:154
  138.1 105.3 %reduce-scatter.2.cloned.1.call-start = ((), (), s32[]{:S(2)}) async-start(), calls=%async_computation.7 | async-start | bytes 8257536 | tf_op jit(solution)/shard_map/reduce_scatter | solution.py:156
  181.7 6.3 %copy-start.1 = (bf16[1,128,7168]{2,1,0:T(8,128)(2,1)S(1)}, bf16[1,128,7168]{2,1,0:T(8,128)(2,1)}, u32[]{:S(2)}) copy-start(bf16[1,128,7168]{2,1,0:T(8,128)(2,1)} %param.23) | copy-start | bytes 5505028
Sparse Core Ops, SparseCore 0:
  21.4 43.7 all-gather.2
  138.3 43.3 all-gather.4
  193.2 50.1 reduce-scatter.1
where the time goes:
time: 294 us; the launch traced here: 293 us
  waiting for transfers between devices  150 us (51%)
  blocking collectives  69.6 us (24%)
  matrix products  23.8 us (8%)
  local copies, waits for them, and re-layouts  22.7 us (8%)
  between operations  14 us (5%)
  starting transfers between devices  10.5 us (4%)
    all_to_all x2, blocking collectives, exchange_both(): tiles = lax.all_to_all(tiles, axis, split_axis=0, concat_axis=0, tiled=True)  62 us
    reduce_scatter x1, waiting for transfers between devices, shards(): lax.psum_scatter(every_out.astype(jnp.float32).astype(jnp.bfloat16), 'tp'...  50.3 us
    all_gather x1, waiting for transfers between devices, shards(): lax.all_gather(local_rows, 'tp', axis=0, tiled=True)  43.3 us
    all_gather x1, waiting for transfers between devices, gathered_by_axis(): out = lax.all_gather(out, axes[number], axis=dim, tiled=True)  35.4 us
    all_to_all x1, waiting for transfers between devices, shards(): lax.all_to_all(column_part, GRP, split_axis=0, concat_axis=2, tiled=True)[0]  10.3 us
    all_to_all x1, waiting for transfers between devices, sent_and_summed(): lax.all_to_all(tiles, axis, split_axis=0, concat_axis=0, tiled=True)  10.1 us
    all_gather x1, blocking collectives, gathered_by_axis(): out = lax.all_gather(out, axes[number], axis=dim, tiled=True)  7.51 us
    dot_general x1, matrix products, expert_slice(): jnp.dot(rows_in, expert_in[0].reshape(width, 2 * slice_width), preferred_...  6.32 us
  transfers between devices with their start and end apart: 5, of which 5 were waited for; matrix products, arithmetic and copies ran while one was open for 3% of the time, Pallas kernels for 0%

commit v1 on v0

--- a/solution.py
+++ b/solution.py
@@ -10,6 +10,13 @@
 SEC_GRP_TP = ("sec", "grp_0", "grp_1", "tp")
 score_scale = 192.0 ** (-0.5)
 route_scale = 2.5
+
+
+def gather_over(shard, axis, dim):
+    size = lax.axis_size(axis)
+    blocks = jnp.stack([shard for _ in range(size)])
+    blocks = lax.all_to_all(blocks, axis, split_axis=0, concat_axis=0)
+    return jnp.concatenate(blocks, axis=dim)
 
 
 def gathered_by_axis(x, axes, dim):
@@ -150,9 +157,7 @@
     once_rows = outgoing.reshape(sections, expert_groups, capacity, width)
     arrived = exchange_both(once_rows, SEC_GRP, ("sec", GRP), (0, 1), (0, 1))
     local_rows = arrived.reshape(-1, width)
-    every_out = expert_slice(
-        lax.all_gather(local_rows, "tp", axis=0, tiled=True), expert_in, expert_out
-    )
+    every_out = expert_slice(gather_over(local_rows, "tp", 0), expert_in, expert_out)
     own_sums = lax.psum_scatter(
         every_out.astype(jnp.float32).astype(jnp.bfloat16), "tp", scatter_dimension=0, tiled=True
     ).astype(jnp.float32)

time: 294 us -> 330 us (1.12)
  blocking collectives: 69.6 us -> 156 us
  waiting for transfers between devices: 150 us -> 102 us
  matrix products: 23.8 us -> 19.6 us
    all_to_all x0 -> x1, blocking collectives: none -> 86.2 us  [gather_over(): blocks = lax.all_to_all(blocks, axis, split_axis=0, concat_axis=0)]
    all_gather x1 -> x0, waiting for transfers between devices: 43.3 us -> none  [shards(): lax.all_gather(local_rows, 'tp', axis=0, tiled=True)]
    dot_general x1, matrix products: 6.32 us -> 2.14 us  [expert_slice(): jnp.dot(rows_in, expert_in[0].reshape(width, 2 * slice_width), preferred_...]
    reduce_scatter x1, waiting for transfers between devices: 50.3 us -> 46.2 us  [shards(): lax.psum_scatter(every_out.astype(jnp.float32).astype(jnp.bfloat16), 'tp'...]
  transfers between devices with their start and end apart: 5 -> 4, of which waited for: 5 -> 4; matrix products, arithmetic and copies ran while one was open for 3% -> 2% of each run, Pallas kernels for 0% -> 0%
where the time goes in v1:
time: 330 us
  blocking collectives  156 us (47%)
  waiting for transfers between devices  102 us (31%)
  local copies, waits for them, and re-layouts  24.8 us (8%)
  matrix products  19.6 us (6%)
  between operations  14.3 us (4%)
  starting transfers between devices  10.2 us (3%)
    all_to_all x1, blocking collectives, gather_over(): blocks = lax.all_to_all(blocks, axis, split_axis=0, concat_axis=0)  86.2 us
    all_to_all x2, blocking collectives, exchange_both(): tiles = lax.all_to_all(tiles, axis, split_axis=0, concat_axis=0, tiled=True)  62 us
    reduce_scatter x1, waiting for transfers between devices, shards(): lax.psum_scatter(every_out.astype(jnp.float32).astype(jnp.bfloat16), 'tp'...  46.2 us
    all_gather x1, waiting for transfers between devices, gathered_by_axis(): out = lax.all_gather(out, axes[number], axis=dim, tiled=True)  35.4 us
    all_to_all x1, waiting for transfers between devices, shards(): lax.all_to_all(column_part, GRP, split_axis=0, concat_axis=2, tiled=True)[0]  10.3 us
    all_to_all x1, waiting for transfers between devices, sent_and_summed(): lax.all_to_all(tiles, axis, split_axis=0, concat_axis=0, tiled=True)  10.1 us
    all_gather x1, blocking collectives, gathered_by_axis(): out = lax.all_gather(out, axes[number], axis=dim, tiled=True)  7.51 us
  transfers between devices with their start and end apart: 4, of which 4 were waited for; matrix products, arithmetic and copies ran while one was open for 2% of the time, Pallas kernels for 0%

profile of v1, /device:TPU:8, one launch (start us, length us, event | category | flops | bytes accessed | tf_op | source)
XLA Modules:
  0.0 329.5 jit_solution(11342503244446615319)
XLA Ops:
  6.5 0.0 copy-start
  6.5 0.0 all-gather.2.cloned.1.call-start
  6.5 0.9 iota_compare_fusion.1
  7.4 2.9 fusion.29
  10.3 0.2 fusion.52
  10.5 2.5 fusion.19
  13.1 0.0 copy-done
  13.1 0.6 fusion.33
  13.7 7.5 %all_gather.6 = bf16[64,2048]{1,0:T(8,128)(2,1)} all-gather(bf16[32,2048]{1,0:T(8,128)(2,1)S(1)} %bitcast.88), channel_id=1, replica_groups=mesh['sec'=2,'grp_0'=8,'grp_1'=2,'tp'=8] {'grp_1'}, dimensions={0}, use_global_device_ids=true | all-gather | bytes 393216 | tf_op jit(solution)/shard_map/all_gather | solution.py:25
  21.3 0.0 all-gather.2.cloned.1.call-update
  21.9 3.9 %copy.34 = bf16[16,1,128,448]{2,0,3,1:T(8,128)(2,1)} copy(bf16[16,1,128,448]{2,3,1,0:T(8,128)(2,1)} %param.17) | data formatting | bytes 3670016 | tf_op args[5]
  25.9 3.9 %reshape.230 = bf16[2048,448,1,1]{0,1,2,3:T(8,128)(2,1)} reshape(bf16[16,1,128,448]{2,0,3,1:T(8,128)(2,1)} %copy.34) | data formatting | bytes 3670016 | tf_op jit(solution)/shard_map/reshape;squeeze | solution.py:112
  29.7 35.4 %all-gather.2.cloned.1.call-done = bf16[512,2048]{1,0:T(8,128)(2,1)} async-done(((bf16[64,2048]{1,0:T(8,128)(2,1)}), bf16[512,2048]{1,0:T(8,128)(2,1)}) %all-gather.2.cloned.1.call-update) | async-done | bytes 2097168 | tf_op jit(solution)/shard_map/all_gather | solution.py:25
  65.2 4.1 %dot_general.32 = bf16[16,8,4,2048]{3,2,1,0:T(4,128)(2,1)} reshape(bf16[512,2048]{1,0:T(8,128)(2,1)} %all-gather.2.cloned.1.call-done) | data formatting | bytes 4194304 | tf_op jit(solution)/shard_map/dot_general | solution.py:113
  69.3 3.6 %fusion.22 = bf16[8,16,1,4,448]{4,0,3,1,2:T(8,128)(2,1)S(1)} fusion(bf16[2048,448,1,1]{0,1,2,3:T(8,128)(2,1)} %reshape.230, bf16[16,8,4,2048]{3,2,1,0:T(4,128)(2,1)} %dot_general.32), kind=kOutput, calls=%fused_computation.19 | convolution fusion | flops 939753472 | bytes 4390912 | tf_op jit(solution)/shard_map/dot_general | solution.py:113
  72.9 0.0 copy-start.4
  72.9 0.0 copy-start.2
  72.9 0.0 copy-start.3
  72.9 1.1 copy.36
  74.0 4.3 %all-to-all-start = ((bf16[8,16,1,4,448]{4,3,1,2,0:T(4,128)(2,1)}), bf16[8,16,1,4,448]{4,3,1,2,0:T(4,128)(2,1)S(1)}, u32[]{:S(2)}, u32[]{:S(2)}) async-start(bf16[8,16,1,4,448]{4,3,1,2,0:T(4,128)(2,1)} %copy.36), calls=%async_computation | async-start | bytes 1048576 | tf_op jit(solution)/shard_map/all_to_all | solution.py:37
  78.2 0.0 copy-done.4
  78.2 0.1 fusion.47
  78.3 0.1 fusion.51
  78.5 10.1 %all-to-all-done = bf16[8,16,1,4,448]{4,3,1,2,0:T(4,128)(2,1)S(1)} async-done(((bf16[8,16,1,4,448]{4,3,1,2,0:T(4,128)(2,1)}), bf16[8,16,1,4,448]{4,3,1,2,0:T(4,128)(2,1)S(1)}, u32[]{:S(2)}, u32[]{:S(2)}) %all-to-all-start) | async-done | bytes 458784 | tf_op jit(solution)/shard_map/all_to_all | solution.py:37
  88.5 0.9 reduce_sum.58
  89.4 5.9 %all-to-all-start.1 = ((bf16[16,4,448]{2,1,0:T(4,128)(2,1)}), bf16[16,4,448]{2,1,0:T(4,128)(2,1)S(1)}, u32[]{:S(2)}, u32[]{:S(2)}) async-start(bf16[16,4,448]{2,1,0:T(4,128)(2,1)} %reduce_sum.58), calls=%async_computation.1 | async-start | bytes 131072 | tf_op jit(solution)/shard_map/all_to_all | solution.py:121
  95.4 0.0 reduce-scatter.2.cloned.1.call-start
  95.4 0.1 copy.39
  95.5 0.1 copy.40
  95.6 10.3 %all-to-all-done.1 = bf16[16,4,448]{2,1,0:T(4,128)(2,1)S(1)} async-done(((bf16[16,4,448]{2,1,0:T(4,128)(2,1)}), bf16[16,4,448]{2,1,0:T(4,128)(2,1)S(1)}, u32[]{:S(2)}, u32[]{:S(2)}) %all-to-all-start.1) | async-done | bytes 57376 | tf_op jit(solution)/shard_map/all_to_all | solution.py:121
  106.0 0.1 reshape.228
  106.1 0.0 copy-done.2
  106.1 0.2 multiply_reduce_fusion
  106.3 0.0 copy-done.3
  106.3 0.1 multiply_convert_fusion
  106.4 1.2 fusion.38
  107.7 0.2 select_reduce_fusion
  107.9 0.1 divide_multiply_fusion
  107.9 0.1 select_reduce_fusion.2
  108.0 0.1 copy.41
  108.2 0.4 fusion.1
  108.6 0.9 copy.43
  109.5 27.3 %all_to_all.29 = bf16[32,1,1,2,7168]{4,3,2,1,0:T(2,128)(2,1)S(1)} all-to-all(bf16[32,1,1,2,7168]{4,3,2,1,0:T(2,128)(2,1)S(1)} %copy.43), channel_id=1, replica_groups=mesh['sec'=2,'grp_0'=8,'grp_1'=2,'tp'=8] {'sec','grp_0','grp_1'}, dimensions={0} | all-to-all | bytes 1835008 | tf_op jit(solution)/shard_map/all_to_all | solution.py:53
  136.9 1.3 stack_reshape_reshape.2
  138.1 2.1 stack.3
  140.2 0.0 copy-start.5
  140.2 86.2 %all_to_all.30 = bf16[8,64,7168]{2,1,0:T(8,128)(2,1)S(1)} all-to-all(bf16[8,64,7168]{2,1,0:T(8,128)(2,1)S(1)} %stack.3), channel_id=1, replica_groups=mesh['sec'=2,'grp_0'=8,'grp_1'=2,'tp'=8] {'tp'}, dimensions={0} | all-to-all | bytes 14680064 | tf_op jit(solution)/shard_map/all_to_all | solution.py:18
  226.4 0.0 copy-done.5
  226.4 0.0 copy-start.1
  226.4 2.1 fusion.3
  228.6 0.0 copy-done.1
  228.6 5.1 %convolution_convert_fusion = bf16[512,7168]{1,0:T(8,128)(2,1)} fusion(bf16[1,128,7168]{2,1,0:T(8,128)(2,1)S(1)} %copy-done.1, f32[512,256]{1,0:T(8,128)S(1)} %fusion.3), kind=kOutput, calls=%fused_computation.1 | convolution fusion | flops 943587328 | bytes 9699328 | tf_op jit(solution)/shard_map/dot_general | solution.py:67
  233.6 0.0 reduce-scatter.2.cloned.1.call-update
  233.6 46.2 %reduce-scatter.2.cloned.1.call-done = bf16[64,7168]{1,0:T(8,128)(2,1)} async-done(((bf16[512,7168]{1,0:T(8,128)(2,1)}), bf16[64,7168]{1,0:T(8,128)(2,1)}) %reduce-scatter.2.cloned.1.call-update) | async-done | bytes 917520 | tf_op jit(solution)/shard_map/reduce_scatter | solution.py:161
  279.8 2.3 convert_element_type.99
  282.2 0.6 copy.44
  282.8 34.7 %all_to_all.31 = bf16[32,1,1,2,7168]{4,3,2,1,0:T(2,128)(2,1)S(1)} all-to-all(bf16[32,1,1,2,7168]{4,3,2,1,0:T(2,128)(2,1)S(1)} %bitcast.85), channel_id=1, replica_groups=mesh['sec'=2,'grp_0'=8,'grp_1'=2,'tp'=8] {'grp_0','grp_1','sec'}, dimensions={0} | all-to-all | bytes 1835008 | tf_op jit(solution)/shard_map/all_to_all | solution.py:53
  317.5 1.6 copy.67
  319.0 2.5 reshape.227
  321.5 1.2 fusion.2
  (8 shorter events, 0.2 us)
Async XLA Ops:
  6.5 6.6 %copy-start = (bf16[16,1,512,128]{3,2,1,0:T(8,128)(2,1)S(1)}, bf16[16,1,512,128]{3,2,1,0:T(8,128)(2,1)}, u32[]{:S(2)}) copy-start(bf16[16,1,512,128]{3,2,1,0:T(8,128)(2,1)} %param.16) | copy-start | bytes 6291460
  6.5 58.6 %all-gather.2.cloned.1.call-start = ((), (), s32[]{:S(2)}) async-start(), calls=%async_computation.6 | async-start | bytes 2359296 | tf_op jit(solution)/shard_map/all_gather | solution.py:25
  72.9 5.4 %copy-start.4 = (s32[4,8]{1,0:T(4,128)S(1)}, s32[4,8]{1,0:T(4,128)}, u32[]{:S(2)}) copy-start(s32[4,8]{1,0:T(4,128)} %param.20) | copy-start | bytes 388
  72.9 33.2 %copy-start.2 = (bf16[4,7168]{1,0:T(4,128)(2,1)S(1)}, bf16[4,7168]{1,0:T(4,128)(2,1)}, u32[]{:S(2)}) copy-start(bf16[4,7168]{1,0:T(4,128)(2,1)} %param.12) | copy-start | bytes 172036
  72.9 33.4 %copy-start.3 = (f32[7168]{0:T(1024)S(1)}, f32[7168]{0:T(1024)}, u32[]{:S(2)}) copy-start(f32[7168]{0:T(1024)} %param.18) | copy-start | bytes 86020
  74.0 14.6 %all-to-all-start = ((bf16[8,16,1,4,448]{4,3,1,2,0:T(4,128)(2,1)}), bf16[8,16,1,4,448]{4,3,1,2,0:T(4,128)(2,1)S(1)}, u32[]{:S(2)}, u32[]{:S(2)}) async-start(bf16[8,16,1,4,448]{4,3,1,2,0:T(4,128)(2,1)} %copy.36), calls=%async_computation | async-start | bytes 1048576 | tf_op jit(solution)/shard_map/all_to_all | solution.py:37
  89.4 16.5 %all-to-all-start.1 = ((bf16[16,4,448]{2,1,0:T(4,128)(2,1)}), bf16[16,4,448]{2,1,0:T(4,128)(2,1)S(1)}, u32[]{:S(2)}, u32[]{:S(2)}) async-start(bf16[16,4,448]{2,1,0:T(4,128)(2,1)} %reduce_sum.58), calls=%async_computation.1 | async-start | bytes 131072 | tf_op jit(solution)/shard_map/all_to_all | solution.py:121
  95.4 184.4 %reduce-scatter.2.cloned.1.call-start = ((), (), s32[]{:S(2)}) async-start(), calls=%async_computation.7 | async-start | bytes 8257536 | tf_op jit(solution)/shard_map/reduce_scatter | solution.py:161
  140.2 86.2 %copy-start.5 = (bf16[1,7168,2,128]{3,2,1,0:T(2,128)(2,1)S(1)}, bf16[1,7168,2,128]{3,2,1,0:T(2,128)(2,1)}, u32[]{:S(2)}) copy-start(bf16[1,7168,2,128]{3,2,1,0:T(2,128)(2,1)} %param.22) | copy-start | bytes 11010052
  226.4 2.2 copy-start.1
Sparse Core Ops, SparseCore 0:
  21.4 43.7 all-gather.1
  233.8 45.9 reduce-scatter.1
